TPU v7x, 256 devices: a whole 4x4x8 slice. The times are simulated.
256 devices in a mesh: rep: 8 (over y, x_hi), blk: 32 (over z, x_lo, core).
Axes of the slice: x: 4 (x_hi: 2, x_lo: 2; x = x_hi * 2 + x_lo), y: 4, z: 8, core: 2. Of those that a mesh axis runs over, the one named last changes fastest.
Arguments:
- features: bfloat16 [131072, 128], P(('rep', 'blk')), may hold values from -6 to 6
- degrees: int32 [131072], P(('rep', 'blk')), may hold values from 1 to 32
- tile_weights: bfloat16 [8, 32, 320, 128, 128], P('rep', 'blk'), may hold values from 0 to 0.049804688
- tile_rows: int32 [8, 32, 320], P('rep', 'blk'), may hold values from 0 to 127, as said below
- tile_cols: int32 [8, 32, 320], P('rep', 'blk'), may hold values from 0 to 31, as said below
- tile_counts: int32 [8, 32], P('rep', 'blk'), may hold values from 1 to 320, as said below
- weight: bfloat16 [128, 256], replicated, may hold values from -0.5 to 0.5
- layer_bias: float32 [256], replicated, may hold values from -3 to 3
- upstream: bfloat16 [131072, 256], P(('rep', 'blk')), may hold values from -6 to 6
Outputs:
- hidden: bfloat16 [131072, 256], P(('rep', 'blk'))
- feature_grad: bfloat16 [131072, 128], P(('rep', 'blk'))
- weight_grad: float32 [128, 256], replicated
- bias_grad: float32 [256], replicated
Inputs may be any that keep to these rules, and one draw needn't show every extreme that they name: `tile_rows`: the first tile_counts slots of a device hold distinct tiles, ordered by row and then by column; a used row h lies in node block r * 32 + h // 4, whose index h // 4 is within 3 steps of the device's blk index around the loop of 32; unused slots hold the device's own first tile row. `tile_cols`: unused slots hold 0. `tile_counts`: at most 80 used slots of one device lie in the rows of one node block; this and the largest count are both reached by some device in every draw.
All inputs are finite; a program needn't handle non-finite values.
Results may differ from a plain program's by a relative error of at most 0.015.
Values may be sent and summed in bfloat16 or wider, within the bound.
A program may use at most 128 MiB of HBM per device.

v0:
```python
import jax
import jax.numpy as jnp
from jax import lax
from jax.sharding import PartitionSpec as P

REACH = 3


def shifted(value, axis, by):
    length = lax.axis_size(axis)
    return lax.ppermute(value, axis, [(i, (i + by) % length) for i in range(length)])


def node_scale(degrees):
    return 1.0 / jnp.sqrt(degrees.astype(jnp.float32) + 1.0)


def on_device(
    features, degrees, tile_weights, tile_rows, tile_cols, tile_counts, weight, layer_bias, upstream
):
    row_count, feat_width = features.shape
    tile_size = tile_weights.shape[-1]
    slot_total = tile_weights.shape[2]
    row_tiles = row_count // tile_size
    rep_count = lax.axis_size("rep")
    blk_count = lax.axis_size("blk")
    blk_index = lax.axis_index("blk")
    window_blocks = 2 * REACH + 1
    window_tiles = window_blocks * row_tiles
    column_tiles = rep_count * row_tiles
    slot_block = slot_total // (2 * (REACH + 1))
    block_total = slot_total // slot_block
    weights_dev = tile_weights[0, 0]
    rows_dev = tile_rows[0, 0]
    cols_dev = tile_cols[0, 0]
    count_dev = tile_counts[0, 0]
    group_index = rows_dev // row_tiles
    distance = (group_index - blk_index) % blk_count
    distance = jnp.where(distance > blk_count // 2, distance - blk_count, distance)
    window_rows = (distance + REACH) * row_tiles + rows_dev % row_tiles
    slot_ids = jnp.arange(slot_total, dtype=jnp.int32)
    slot_valid = slot_ids < count_dev
    window_seg = jnp.where(slot_valid, window_rows, window_tiles)
    column_seg = jnp.where(slot_valid, cols_dev, column_tiles)

    def tile_pass(source_tiles, gather_index, segment_index, segment_total, pattern):

        def add_block(block_id, running):
            slot_first = block_id * slot_block
            weights_part = lax.dynamic_slice_in_dim(weights_dev, slot_first, slot_block, 0)
            gather_part = lax.dynamic_slice_in_dim(gather_index, slot_first, slot_block, 0)
            segment_part = lax.dynamic_slice_in_dim(segment_index, slot_first, slot_block, 0)
            products = jnp.einsum(
                pattern, weights_part, source_tiles[gather_part], preferred_element_type=jnp.float32
            )
            return (
                running
                + jax.ops.segment_sum(products, segment_part, segment_total + 1)[:segment_total]
            )

        zero_sum = jnp.zeros((segment_total, tile_size, feat_width), jnp.float32)
        return lax.fori_loop(0, block_total, add_block, zero_sum)

    node_norm = node_scale(degrees)
    scaled = (node_norm[:, None] * features.astype(jnp.float32)).astype(jnp.bfloat16)
    source_rows = lax.all_gather(scaled, "rep", axis=0, tiled=True)
    source_tiles = source_rows.reshape(column_tiles, tile_size, feat_width)
    partial_value = tile_pass(source_tiles, cols_dev, window_seg, window_tiles, "tab,tbf->taf")
    partial_value = partial_value.reshape(window_blocks, row_count, feat_width)
    neighbor_sum = partial_value[REACH]
    for offset in range(-REACH, REACH + 1):
        if offset != 0:
            neighbor_sum = neighbor_sum + shifted(
                partial_value[offset + REACH].astype(jnp.bfloat16), "blk", offset
            ).astype(jnp.float32)
    aggregated = (node_norm[:, None] * (neighbor_sum + scaled.astype(jnp.float32))).astype(
        jnp.bfloat16
    )
    pre_act = jnp.dot(aggregated, weight, preferred_element_type=jnp.float32) + layer_bias
    hidden = jax.nn.silu(pre_act).astype(jnp.bfloat16)
    gate_sigmoid = jax.nn.sigmoid(pre_act)
    pre_grad = (
        upstream.astype(jnp.float32)
        * (gate_sigmoid + pre_act * gate_sigmoid * (1.0 - gate_sigmoid))
    ).astype(jnp.bfloat16)
    local_weight = jnp.dot(aggregated.T, pre_grad, preferred_element_type=jnp.float32)
    local_bias = jnp.sum(pre_grad.astype(jnp.float32), axis=0)
    weight_sum, bias_sum = lax.psum((local_weight, local_bias), ("rep", "blk"))
    grad_scale = (row_count * rep_count * blk_count) ** (-0.5)
    scaled_grad = (
        node_norm[:, None] * jnp.dot(pre_grad, weight.T, preferred_element_type=jnp.float32)
    ).astype(jnp.bfloat16)
    window_parts = [scaled_grad] * window_blocks
    for offset in range(-REACH, REACH + 1):
        if offset != 0:
            window_parts[offset + REACH] = shifted(scaled_grad, "blk", -offset)
    grad_tiles = jnp.stack(window_parts).reshape(window_tiles, tile_size, feat_width)
    column_part = tile_pass(grad_tiles, window_rows, column_seg, column_tiles, "tab,taf->tbf")
    column_sum = lax.psum_scatter(
        column_part.reshape(rep_count * row_count, feat_width).astype(jnp.bfloat16),
        "rep",
        scatter_dimension=0,
        tiled=True,
    ).astype(jnp.float32)
    feature_grad = (node_norm[:, None] * (column_sum + scaled_grad.astype(jnp.float32))).astype(
        jnp.bfloat16
    )
    return (hidden, feature_grad, weight_sum * grad_scale, bias_sum * grad_scale)


def solution(mesh):
    placed = (
        P(("rep", "blk"), None),
        P(("rep", "blk")),
        P("rep", "blk", None, None, None),
        P("rep", "blk", None),
        P("rep", "blk", None),
        P("rep", "blk"),
        P(),
        P(),
        P(("rep", "blk"), None),
    )
    return jax.shard_map(
        on_device,
        mesh=mesh,
        in_specs=placed,
        out_specs=(P(("rep", "blk"), None), P(("rep", "blk"), None), P(), P()),
        check_vma=False,
    )
```

profile of v0, /device:TPU:32, one launch (start us, length us, event | category | flops | bytes accessed | tf_op | source)
XLA Modules:
  0.0 557.3 jit_solution(4385618830677992955)
XLA Ops:
  11.8 53.4 %all-gather.2.cloned.1.call-done = bf16[4096,128]{1,0:T(8,128)(2,1)} async-done(((bf16[512,128]{1,0:T(8,128)(2,1)}), bf16[4096,128]{1,0:T(8,128)(2,1)}) %all-gather.2.cloned.1.call-update) | async-done | bytes 1048592 | tf_op jit(solution)/shard_map/all_gather | solution.py:66
  65.2 120.4 %while.28 = (s32[]{:T(128)}, f32[28,128,128]{2,1,0:T(8,128)}, s32[320]{0:T(512)S(1)}, bf16[320,128,128]{2,1,0:T(8,128)(2,1)}, s32[320]{0:T(512)S(1)}, /*index=5*...) while((s32[]{:T(128)}, f32[28,128,128]{2,1,0:T(8,128)}, ...), condition=%wide.region_2.3_spmd.clone, body=%wide.region_0.2_spmd.clone.sunk | while | flops 169346176 | bytes 23139612 | solution.py:62
  67.4 3.3 fusion.44
  71.0 6.5 %scatter_fusion = f32[29,128,128]{2,1,0:T(8,128)S(1)} fusion(f32[29,128,128]{2,1,0:T(8,128)S(1)} %broadcast.127, s32[40]{0:T(128)S(1)} %dynamic_slice.62, f32[40,128,128]{2,1,0:T(8,128)} %fusion.44), kind=kCustom, calls=%fused_computation.2.clone.clone.1 | custom fusion | flops 655360 | bytes 7864480 | tf_op jit(solution)/shard_map/while/body/eval_jaxpr/scatter-add | solution.py:58
  79.1 2.0 gather_fusion
  81.2 3.3 fusion.44
  84.7 6.5 %scatter_fusion = f32[29,128,128]{2,1,0:T(8,128)S(1)} fusion(f32[29,128,128]{2,1,0:T(8,128)S(1)} %broadcast.127, s32[40]{0:T(128)S(1)} %dynamic_slice.62, f32[40,128,128]{2,1,0:T(8,128)} %fusion.44), kind=kCustom, calls=%fused_computation.2.clone.clone.1 | custom fusion | flops 655360 | bytes 7864480 | tf_op jit(solution)/shard_map/while/body/eval_jaxpr/scatter-add | solution.py:58
  91.3 3.0 slice_add_fusion.4
  96.4 3.3 fusion.44
  100.0 6.5 %scatter_fusion = f32[29,128,128]{2,1,0:T(8,128)S(1)} fusion(f32[29,128,128]{2,1,0:T(8,128)S(1)} %broadcast.127, s32[40]{0:T(128)S(1)} %dynamic_slice.62, f32[40,128,128]{2,1,0:T(8,128)} %fusion.44), kind=kCustom, calls=%fused_computation.2.clone.clone.1 | custom fusion | flops 655360 | bytes 7864480 | tf_op jit(solution)/shard_map/while/body/eval_jaxpr/scatter-add | solution.py:58
  106.5 3.0 slice_add_fusion.4
  109.6 2.0 gather_fusion
  111.6 3.3 fusion.44
  115.2 6.5 %scatter_fusion = f32[29,128,128]{2,1,0:T(8,128)S(1)} fusion(f32[29,128,128]{2,1,0:T(8,128)S(1)} %broadcast.127, s32[40]{0:T(128)S(1)} %dynamic_slice.62, f32[40,128,128]{2,1,0:T(8,128)} %fusion.44), kind=kCustom, calls=%fused_computation.2.clone.clone.1 | custom fusion | flops 655360 | bytes 7864480 | tf_op jit(solution)/shard_map/while/body/eval_jaxpr/scatter-add | solution.py:58
  121.7 3.0 slice_add_fusion.4
  126.9 3.3 fusion.44
  130.4 6.5 %scatter_fusion = f32[29,128,128]{2,1,0:T(8,128)S(1)} fusion(f32[29,128,128]{2,1,0:T(8,128)S(1)} %broadcast.127, s32[40]{0:T(128)S(1)} %dynamic_slice.62, f32[40,128,128]{2,1,0:T(8,128)} %fusion.44), kind=kCustom, calls=%fused_computation.2.clone.clone.1 | custom fusion | flops 655360 | bytes 7864480 | tf_op jit(solution)/shard_map/while/body/eval_jaxpr/scatter-add | solution.py:58
  137.0 3.0 slice_add_fusion.4
  140.1 2.0 gather_fusion
  142.1 3.3 fusion.44
  145.7 6.5 %scatter_fusion = f32[29,128,128]{2,1,0:T(8,128)S(1)} fusion(f32[29,128,128]{2,1,0:T(8,128)S(1)} %broadcast.127, s32[40]{0:T(128)S(1)} %dynamic_slice.62, f32[40,128,128]{2,1,0:T(8,128)} %fusion.44), kind=kCustom, calls=%fused_computation.2.clone.clone.1 | custom fusion | flops 655360 | bytes 7864480 | tf_op jit(solution)/shard_map/while/body/eval_jaxpr/scatter-add | solution.py:58
  152.2 3.0 slice_add_fusion.4
  155.3 2.0 gather_fusion
  157.4 3.3 fusion.44
  160.9 6.5 %scatter_fusion = f32[29,128,128]{2,1,0:T(8,128)S(1)} fusion(f32[29,128,128]{2,1,0:T(8,128)S(1)} %broadcast.127, s32[40]{0:T(128)S(1)} %dynamic_slice.62, f32[40,128,128]{2,1,0:T(8,128)} %fusion.44), kind=kCustom, calls=%fused_computation.2.clone.clone.1 | custom fusion | flops 655360 | bytes 7864480 | tf_op jit(solution)/shard_map/while/body/eval_jaxpr/scatter-add | solution.py:58
  167.5 3.0 slice_add_fusion.4
  172.6 3.3 fusion.44
  176.2 6.5 %scatter_fusion = f32[29,128,128]{2,1,0:T(8,128)S(1)} fusion(f32[29,128,128]{2,1,0:T(8,128)S(1)} %broadcast.127, s32[40]{0:T(128)S(1)} %dynamic_slice.62, f32[40,128,128]{2,1,0:T(8,128)} %fusion.44), kind=kCustom, calls=%fused_computation.2.clone.clone.1 | custom fusion | flops 655360 | bytes 7864480 | tf_op jit(solution)/shard_map/while/body/eval_jaxpr/scatter-add | solution.py:58
  182.7 3.0 slice_add_fusion.4
  187.5 14.4 %copy.13 = bf16[1,1,320,128,128]{3,4,2,1,0:T(8,128)(2,1)} copy(bf16[1,1,320,128,128]{4,3,2,1,0:T(8,128)(2,1)} %bitcast.61) | data formatting | bytes 20971520 | tf_op args[2]
  204.2 2.6 collective-permute-start.2
  209.3 4.0 collective-permute-done.4
  213.3 2.2 collective-permute-done.1
  219.0 3.3 collective-permute-start.9
  223.9 5.1 collective-permute-done.6
  230.9 5.0 collective-permute-done.7
  236.2 113.0 %while.29 = (s32[]{:T(128)}, f32[32,128,128]{2,1,0:T(8,128)}, s32[320]{0:T(512)S(1)}, bf16[320,128,128]{1,2,0:T(8,128)(2,1)}, s32[320]{0:T(512)S(1)}, /*index=5*...) while((s32[]{:T(128)}, f32[32,128,128]{2,1,0:T(8,128)}, ...), condition=%wide.region_5.6_spmd.clone, body=%wide.region_3.5_spmd.clone.sunk | while | flops 169477248 | bytes 24188188 | solution.py:62
  237.2 3.3 fusion.47
  240.7 6.6 %scatter_fusion.1 = f32[33,128,128]{2,1,0:T(8,128)S(1)} fusion(f32[33,128,128]{2,1,0:T(8,128)S(1)} %broadcast.134, s32[40]{0:T(128)S(1)} %dynamic_slice.65, f32[40,128,128]{2,1,0:T(8,128)} %fusion.47), kind=kCustom, calls=%fused_computation.3.clone.clone.1 | custom fusion | flops 655360 | bytes 7864480 | tf_op jit(solution)/shard_map/while/body/eval_jaxpr/scatter-add | solution.py:58
  249.9 3.3 fusion.47
  253.5 6.6 %scatter_fusion.1 = f32[33,128,128]{2,1,0:T(8,128)S(1)} fusion(f32[33,128,128]{2,1,0:T(8,128)S(1)} %broadcast.134, s32[40]{0:T(128)S(1)} %dynamic_slice.65, f32[40,128,128]{2,1,0:T(8,128)} %fusion.47), kind=kCustom, calls=%fused_computation.3.clone.clone.1 | custom fusion | flops 655360 | bytes 7864480 | tf_op jit(solution)/shard_map/while/body/eval_jaxpr/scatter-add | solution.py:58
  260.1 3.2 slice_add_fusion.5
  264.2 3.3 fusion.47
  267.8 6.6 %scatter_fusion.1 = f32[33,128,128]{2,1,0:T(8,128)S(1)} fusion(f32[33,128,128]{2,1,0:T(8,128)S(1)} %broadcast.134, s32[40]{0:T(128)S(1)} %dynamic_slice.65, f32[40,128,128]{2,1,0:T(8,128)} %fusion.47), kind=kCustom, calls=%fused_computation.3.clone.clone.1 | custom fusion | flops 655360 | bytes 7864480 | tf_op jit(solution)/shard_map/while/body/eval_jaxpr/scatter-add | solution.py:58
  274.4 3.2 slice_add_fusion.5
  278.6 3.3 fusion.47
  282.2 6.6 %scatter_fusion.1 = f32[33,128,128]{2,1,0:T(8,128)S(1)} fusion(f32[33,128,128]{2,1,0:T(8,128)S(1)} %broadcast.134, s32[40]{0:T(128)S(1)} %dynamic_slice.65, f32[40,128,128]{2,1,0:T(8,128)} %fusion.47), kind=kCustom, calls=%fused_computation.3.clone.clone.1 | custom fusion | flops 655360 | bytes 7864480 | tf_op jit(solution)/shard_map/while/body/eval_jaxpr/scatter-add | solution.py:58
  288.7 3.2 slice_add_fusion.5
  292.9 3.3 fusion.47
  296.5 6.6 %scatter_fusion.1 = f32[33,128,128]{2,1,0:T(8,128)S(1)} fusion(f32[33,128,128]{2,1,0:T(8,128)S(1)} %broadcast.134, s32[40]{0:T(128)S(1)} %dynamic_slice.65, f32[40,128,128]{2,1,0:T(8,128)} %fusion.47), kind=kCustom, calls=%fused_computation.3.clone.clone.1 | custom fusion | flops 655360 | bytes 7864480 | tf_op jit(solution)/shard_map/while/body/eval_jaxpr/scatter-add | solution.py:58
  303.1 3.2 slice_add_fusion.5
  307.2 3.3 fusion.47
  310.8 6.6 %scatter_fusion.1 = f32[33,128,128]{2,1,0:T(8,128)S(1)} fusion(f32[33,128,128]{2,1,0:T(8,128)S(1)} %broadcast.134, s32[40]{0:T(128)S(1)} %dynamic_slice.65, f32[40,128,128]{2,1,0:T(8,128)} %fusion.47), kind=kCustom, calls=%fused_computation.3.clone.clone.1 | custom fusion | flops 655360 | bytes 7864480 | tf_op jit(solution)/shard_map/while/body/eval_jaxpr/scatter-add | solution.py:58
  317.4 3.2 slice_add_fusion.5
  321.6 3.3 fusion.47
  325.1 6.5 %scatter_fusion.1 = f32[33,128,128]{2,1,0:T(8,128)S(1)} fusion(f32[33,128,128]{2,1,0:T(8,128)S(1)} %broadcast.134, s32[40]{0:T(128)S(1)} %dynamic_slice.65, f32[40,128,128]{2,1,0:T(8,128)} %fusion.47), kind=kCustom, calls=%fused_computation.3.clone.clone.1 | custom fusion | flops 655360 | bytes 7864480 | tf_op jit(solution)/shard_map/while/body/eval_jaxpr/scatter-add | solution.py:58
  331.7 3.2 slice_add_fusion.5
  335.8 3.3 fusion.47
  339.4 6.5 %scatter_fusion.1 = f32[33,128,128]{2,1,0:T(8,128)S(1)} fusion(f32[33,128,128]{2,1,0:T(8,128)S(1)} %broadcast.134, s32[40]{0:T(128)S(1)} %dynamic_slice.65, f32[40,128,128]{2,1,0:T(8,128)} %fusion.47), kind=kCustom, calls=%fused_computation.3.clone.clone.1 | custom fusion | flops 655360 | bytes 7864480 | tf_op jit(solution)/shard_map/while/body/eval_jaxpr/scatter-add | solution.py:58
  346.0 3.2 slice_add_fusion.5
  349.2 2.7 convert_element_type.108
  351.9 75.9 %psum.15 = f32[256]{0:T(256)S(1)} all-reduce(f32[256]{0:T(256)S(1)} %get-tuple-element.296), channel_id=1, replica_groups=mesh['rep'=8,'blk'=32] {'rep','blk'}, use_global_device_ids=true, to_apply=%region_9.10 | all-reduce | flops 256 | bytes 2048 | tf_op jit(solution)/shard_map/psum | solution.py:88
  428.4 41.1 %all-reduce.2.cloned.1.call-done = f32[128,256]{1,0:T(8,128)} async-done(((f32[128,256]{1,0:T(8,128)}), f32[128,256]{1,0:T(8,128)}) %all-reduce.2.cloned.1.call-update) | async-done | bytes 131088 | tf_op jit(solution)/shard_map/psum | solution.py:88
  471.1 77.9 %reduce-scatter.2.cloned.1.call-done = bf16[512,128]{1,0:T(8,128)(2,1)} async-done(((bf16[4096,128]{1,0:T(8,128)(2,1)}), bf16[512,128]{1,0:T(8,128)(2,1)}) %reduce-scatter.2.cloned.1.call-update) | async-done | bytes 131088 | tf_op jit(solution)/shard_map/reduce_scatter | solution.py:99
  (135 shorter events, 45.0 us)
Async XLA Ops:
  7.2 208.5 %copy-start = (bf16[128,256]{1,0:T(8,128)(2,1)S(1)}, bf16[128,256]{1,0:T(8,128)(2,1)}, u32[]{:S(2)}) copy-start(bf16[128,256]{1,0:T(8,128)(2,1)} %param.19) | copy-start | bytes 196612
  7.2 58.0 %all-gather.2.cloned.1.call-start = ((), (), s32[]{:S(2)}) async-start(), calls=%async_computation.1 | async-start | bytes 1179648 | tf_op jit(solution)/shard_map/all_gather | solution.py:66
  9.6 459.9 %all-reduce.2.cloned.1.call-start = ((), (), s32[]{:S(2)}) async-start(), calls=%async_computation.3 | async-start | bytes 262144 | tf_op jit(solution)/shard_map/psum | solution.py:88
  187.4 19.5 %collective-permute-start.5 = (bf16[512,128]{1,0:T(8,128)(2,1)S(1)}, bf16[512,128]{1,0:T(8,128)(2,1)S(1)}, u32[]{:S(2)}, u32[]{:S(2)}) collective-permute-start(bf16[512,128]{1,0:T(8,128)(2,1)S(1)} %bitcast.69), channel_id=1, source_target_pairs={{0,3},{1,4},{2,5},{3,6},{4,7},{5,8},{6,9},{7,10},{8,11},{9,12},{10... | collective-permute-start | bytes 393224 | tf_op jit(solution)/shard_map/ppermute | solution.py:11
  187.5 28.0 %copy-start.1 = (bf16[512,128]{1,0:T(8,128)(2,1)S(1)}, bf16[512,128]{1,0:T(8,128)(2,1)}, u32[]{:S(2)}) copy-start(bf16[512,128]{1,0:T(8,128)(2,1)} %param.13) | copy-start | bytes 393220
  187.5 28.2 %copy-start.2 = (bf16[512,256]{1,0:T(8,128)(2,1)S(1)}, bf16[512,256]{1,0:T(8,128)(2,1)}, u32[]{:S(2)}) copy-start(bf16[512,256]{1,0:T(8,128)(2,1)} %param.21) | copy-start | bytes 786436
  187.5 28.2 %copy-start.3 = (f32[256]{0:T(256)S(1)}, f32[256]{0:T(256)}, u32[]{:S(2)}) copy-start(f32[256]{0:T(256)} %param.20) | copy-start | bytes 3076
  201.9 7.3 %collective-permute-start = (bf16[512,128]{1,0:T(8,128)(2,1)S(1)}, bf16[512,128]{1,0:T(8,128)(2,1)S(1)}, u32[]{:S(2)}, u32[]{:S(2)}) collective-permute-start(bf16[512,128]{1,0:T(8,128)(2,1)S(1)} %bitcast.68), channel_id=1, source_target_pairs={{0,29},{1,30},{2,31},{3,0},{4,1},{5,2},{6,3},{7,4},{8,5},{9,6},{10... | collective-permute-start | bytes 393224 | tf_op jit(solution)/shard_map/ppermute | solution.py:11
  203.6 9.7 %collective-permute-start.4 = (bf16[512,128]{1,0:T(8,128)(2,1)S(1)}, bf16[512,128]{1,0:T(8,128)(2,1)S(1)}, u32[]{:S(2)}, u32[]{:S(2)}) collective-permute-start(bf16[512,128]{1,0:T(8,128)(2,1)S(1)} %bitcast.67), channel_id=1, source_target_pairs={{0,2},{1,3},{2,4},{3,5},{4,6},{5,7},{6,8},{7,9},{8,10},{9,11},{10,... | collective-permute-start | bytes 393224 | tf_op jit(solution)/shard_map/ppermute | solution.py:11
  204.2 9.1 %collective-permute-start.3 = (bf16[512,128]{1,0:T(8,128)(2,1)S(1)}, bf16[512,128]{1,0:T(8,128)(2,1)S(1)}, u32[]{:S(2)}, u32[]{:S(2)}) collective-permute-start(bf16[512,128]{1,0:T(8,128)(2,1)S(1)} %bitcast.66), channel_id=1, source_target_pairs={{0,1},{1,2},{2,3},{3,4},{4,5},{5,6},{6,7},{7,8},{8,9},{9,10},{10,1... | collective-permute-start | bytes 393224 | tf_op jit(solution)/shard_map/ppermute | solution.py:11
  204.2 9.1 %collective-permute-start.2 = (bf16[512,128]{1,0:T(8,128)(2,1)S(1)}, bf16[512,128]{1,0:T(8,128)(2,1)S(1)}, u32[]{:S(2)}, u32[]{:S(2)}) collective-permute-start(bf16[512,128]{1,0:T(8,128)(2,1)S(1)} %bitcast.65), channel_id=1, source_target_pairs={{0,31},{1,0},{2,1},{3,2},{4,3},{5,4},{6,5},{7,6},{8,7},{9,8},{10,9... | collective-permute-start | bytes 393224 | tf_op jit(solution)/shard_map/ppermute | solution.py:11
  206.9 8.6 %collective-permute-start.1 = (bf16[512,128]{1,0:T(8,128)(2,1)S(1)}, bf16[512,128]{1,0:T(8,128)(2,1)S(1)}, u32[]{:S(2)}, u32[]{:S(2)}) collective-permute-start(bf16[512,128]{1,0:T(8,128)(2,1)S(1)} %bitcast.64), channel_id=1, source_target_pairs={{0,30},{1,31},{2,0},{3,1},{4,2},{5,3},{6,4},{7,5},{8,6},{9,7},{10,... | collective-permute-start | bytes 393224 | tf_op jit(solution)/shard_map/ppermute | solution.py:11
  217.0 19.1 %collective-permute-start.11 = (bf16[512,128]{1,0:T(8,128)(2,1)S(1)}, bf16[512,128]{1,0:T(8,128)(2,1)S(1)}, u32[]{:S(2)}, u32[]{:S(2)}) collective-permute-start(bf16[512,128]{1,0:T(8,128)(2,1)S(1)} %fusion.6), channel_id=1, source_target_pairs={{0,29},{1,30},{2,31},{3,0},{4,1},{5,2},{6,3},{7,4},{8,5},{9,6},{10... | collective-permute-start | bytes 393224 | tf_op jit(solution)/shard_map/ppermute | solution.py:11
  217.9 18.2 %collective-permute-start.10 = (bf16[512,128]{1,0:T(8,128)(2,1)S(1)}, bf16[512,128]{1,0:T(8,128)(2,1)S(1)}, u32[]{:S(2)}, u32[]{:S(2)}) collective-permute-start(bf16[512,128]{1,0:T(8,128)(2,1)S(1)} %fusion.6), channel_id=1, source_target_pairs={{0,30},{1,31},{2,0},{3,1},{4,2},{5,3},{6,4},{7,5},{8,6},{9,7},{10,... | collective-permute-start | bytes 393224 | tf_op jit(solution)/shard_map/ppermute | solution.py:11
  219.0 17.1 %collective-permute-start.9 = (bf16[512,128]{1,0:T(8,128)(2,1)S(1)}, bf16[512,128]{1,0:T(8,128)(2,1)S(1)}, u32[]{:S(2)}, u32[]{:S(2)}) collective-permute-start(bf16[512,128]{1,0:T(8,128)(2,1)S(1)} %fusion.6), channel_id=1, source_target_pairs={{0,31},{1,0},{2,1},{3,2},{4,3},{5,4},{6,5},{7,6},{8,7},{9,8},{10,9... | collective-permute-start | bytes 393224 | tf_op jit(solution)/shard_map/ppermute | solution.py:11
  222.3 13.7 %collective-permute-start.8 = (bf16[512,128]{1,0:T(8,128)(2,1)S(1)}, bf16[512,128]{1,0:T(8,128)(2,1)S(1)}, u32[]{:S(2)}, u32[]{:S(2)}) collective-permute-start(bf16[512,128]{1,0:T(8,128)(2,1)S(1)} %fusion.6), channel_id=1, source_target_pairs={{0,1},{1,2},{2,3},{3,4},{4,5},{5,6},{6,7},{7,8},{8,9},{9,10},{10,1... | collective-permute-start | bytes 393224 | tf_op jit(solution)/shard_map/ppermute | solution.py:11
  222.3 6.7 %collective-permute-start.6 = (bf16[512,128]{1,0:T(8,128)(2,1)S(1)}, bf16[512,128]{1,0:T(8,128)(2,1)S(1)}, u32[]{:S(2)}, u32[]{:S(2)}) collective-permute-start(bf16[512,128]{1,0:T(8,128)(2,1)S(1)} %fusion.6), channel_id=1, source_target_pairs={{0,3},{1,4},{2,5},{3,6},{4,7},{5,8},{6,9},{7,10},{8,11},{9,12},{10... | collective-permute-start | bytes 393224 | tf_op jit(solution)/shard_map/ppermute | solution.py:11
  223.9 325.1 %reduce-scatter.2.cloned.1.call-start = ((), (), s32[]{:S(2)}) async-start(), calls=%async_computation.2 | async-start | bytes 1179648 | tf_op jit(solution)/shard_map/reduce_scatter | solution.py:99
  229.0 7.0 %collective-permute-start.7 = (bf16[512,128]{1,0:T(8,128)(2,1)S(1)}, bf16[512,128]{1,0:T(8,128)(2,1)S(1)}, u32[]{:S(2)}, u32[]{:S(2)}) collective-permute-start(bf16[512,128]{1,0:T(8,128)(2,1)S(1)} %fusion.6), channel_id=1, source_target_pairs={{0,2},{1,3},{2,4},{3,5},{4,6},{5,7},{6,8},{7,9},{8,10},{9,11},{10,... | collective-permute-start | bytes 393224 | tf_op jit(solution)/shard_map/ppermute | solution.py:11
Sparse Core Ops, SparseCore 0:
  11.2 53.9 all-gather.1
  224.0 245.4 all-reduce.1
  473.4 75.5 reduce-scatter.1
where the time goes:
time: 561 us; the launch traced here: 557 us
  waiting for transfers between devices  189 us (34%)
  other arithmetic  164 us (29%)
  blocking collectives  75.9 us (14%)
  matrix products  55.7 us (10%)
  local copies, waits for them, and re-layouts  42.9 us (8%)
  between operations  14.6 us (3%)
  starting transfers between devices  14.4 us (3%)
    scatter-add x16, other arithmetic, add_block(): jax.ops.segment_sum(products, segment_part, segment_total + 1)  105 us
    reduce_scatter x1, waiting for transfers between devices, on_device(): lax.psum_scatter(column_part.reshape(rep_count * row_count, feat_width).a...  77.9 us
    psum x1, blocking collectives, on_device(): weight_sum, bias_sum = lax.psum((local_weight, local_bias), ('rep', 'blk'))  75.9 us
    dot_general x16, matrix products, add_block(): jnp.einsum(pattern, weights_part, source_tiles[gather_part], preferred_el...  53.5 us
    all_gather x1, waiting for transfers between devices, on_device(): source_rows = lax.all_gather(scaled, 'rep', axis=0, tiled=True)  53.4 us
    add x16, other arithmetic, add_block(): running + jax.ops.segment_sum(products, segment_part, segment_total + 1)[...  46.3 us
    psum x1, waiting for transfers between devices, on_device(): weight_sum, bias_sum = lax.psum((local_weight, local_bias), ('rep', 'blk'))  41.1 us
    gather x16, local copies, waits for them, and re-layouts, add_block(): source_tiles[gather_part]  22.5 us
  transfers between devices with their start and end apart: 15, of which 7 were waited for; matrix products, arithmetic and copies ran while one was open for 24% of the time, Pallas kernels for 0%

commit v1 on v0

--- a/solution.py
+++ b/solution.py
@@ -63,7 +63,9 @@
 
     node_norm = node_scale(degrees)
     scaled = (node_norm[:, None] * features.astype(jnp.float32)).astype(jnp.bfloat16)
-    source_rows = lax.all_gather(scaled, "rep", axis=0, tiled=True)
+    source_rows = jnp.concatenate(
+        lax.all_to_all(jnp.stack([scaled] * lax.axis_size("rep")), "rep", 0, 0), axis=0
+    )
     source_tiles = source_rows.reshape(column_tiles, tile_size, feat_width)
     partial_value = tile_pass(source_tiles, cols_dev, window_seg, window_tiles, "tab,tbf->taf")
     partial_value = partial_value.reshape(window_blocks, row_count, feat_width)

time: 561 us -> 445 us (0.79)
  waiting for transfers between devices: 189 us -> 69.9 us
  starting transfers between devices: 14.4 us -> 24.7 us
  local copies, waits for them, and re-layouts: 42.9 us -> 34.2 us
    reduce_scatter x1, waiting for transfers between devices: 77.9 us -> 0.01 us  [on_device(): lax.psum_scatter(column_part.reshape(rep_count * row_count, feat_width).a...]
    all_gather x1 -> x0, waiting for transfers between devices: 53.4 us -> none  [on_device(): source_rows = lax.all_gather(scaled, 'rep', axis=0, tiled=True)]
    all_to_all x0 -> x1, waiting for transfers between devices: none -> 16.4 us  [on_device(): lax.all_to_all(jnp.stack([scaled] * lax.axis_size('rep')), 'rep', 0, 0)]
    gather x16, local copies, waits for them, and re-layouts: 22.5 us -> 12.8 us  [add_block(): source_tiles[gather_part]]
    all_to_all x0 -> x1, starting transfers between devices: none -> 6.93 us  [on_device(): lax.all_to_all(jnp.stack([scaled] * lax.axis_size('rep')), 'rep', 0, 0)]
    unnamed x15 -> x19, local copies, waits for them, and re-layouts: 14.6 us -> 14.6 us
  transfers between devices with their start and end apart: 15 -> 15, of which waited for: 7 -> 6; matrix products, arithmetic and copies ran while one was open for 24% -> 31% of each run, Pallas kernels for 0% -> 0%
where the time goes in v1:
time: 445 us; the launch traced here: 440 us
  other arithmetic  162 us (36%)
  blocking collectives  75.7 us (17%)
  waiting for transfers between devices  69.9 us (16%)
  matrix products  55.7 us (13%)
  local copies, waits for them, and re-layouts  34.2 us (8%)
  starting transfers between devices  24.7 us (6%)
  between operations  16.4 us (4%)
    scatter-add x16, other arithmetic, add_block(): jax.ops.segment_sum(products, segment_part, segment_total + 1)  105 us
    psum x1, blocking collectives, on_device(): weight_sum, bias_sum = lax.psum((local_weight, local_bias), ('rep', 'blk'))  75.7 us
    dot_general x16, matrix products, add_block(): jnp.einsum(pattern, weights_part, source_tiles[gather_part], preferred_el...  53.5 us
    add x16, other arithmetic, add_block(): running + jax.ops.segment_sum(products, segment_part, segment_total + 1)[...  46.3 us
    psum x1, waiting for transfers between devices, on_device(): weight_sum, bias_sum = lax.psum((local_weight, local_bias), ('rep', 'blk'))  38.9 us
    ppermute x12, starting transfers between devices, shifted(): lax.ppermute(value, axis, [(i, (i + by) % length) for i in range(length)])  17.7 us
    all_to_all x1, waiting for transfers between devices, on_device(): lax.all_to_all(jnp.stack([scaled] * lax.axis_size('rep')), 'rep', 0, 0)  16.4 us
    ppermute x12, waiting for transfers between devices, shifted(): lax.ppermute(value, axis, [(i, (i + by) % length) for i in range(length)])  14.6 us
  transfers between devices with their start and end apart: 15, of which 6 were waited for; matrix products, arithmetic and copies ran while one was open for 31% of the time, Pallas kernels for 0%

profile of v1, /device:TPU:32, one launch (start us, length us, event | category | flops | bytes accessed | tf_op | source)
XLA Modules:
  0.0 439.5 jit_solution(10149008281035345085)
XLA Ops:
  10.9 6.9 %all-to-all-start = ((bf16[8,512,128]{2,1,0:T(8,128)(2,1)}), bf16[8,512,128]{2,1,0:T(8,128)(2,1)S(1)}, u32[]{:S(2)}, u32[]{:S(2)}) async-start(bf16[8,512,128]{2,1,0:T(8,128)(2,1)} %stack.35), calls=%async_computation | async-start | bytes 2097152 | tf_op jit(solution)/shard_map/all_to_all | solution.py:67
  18.6 16.4 %all-to-all-done = bf16[8,512,128]{2,1,0:T(8,128)(2,1)S(1)} async-done(((bf16[8,512,128]{2,1,0:T(8,128)(2,1)}), bf16[8,512,128]{2,1,0:T(8,128)(2,1)S(1)}, u32[]{:S(2)}, u32[]{:S(2)}) %all-to-all-start) | async-done | bytes 1048608 | tf_op jit(solution)/shard_map/all_to_all | solution.py:67
  35.0 110.7 %while.28 = (s32[]{:T(128)}, f32[28,128,128]{2,1,0:T(8,128)}, s32[320]{0:T(512)S(1)}, bf16[320,128,128]{2,1,0:T(8,128)(2,1)}, s32[320]{0:T(512)S(1)}, /*index=5*...) while((s32[]{:T(128)}, f32[28,128,128]{2,1,0:T(8,128)}, ...), condition=%wide.region_2.3_spmd.clone, body=%wide.region_0.2_spmd.clone.sunk | while | flops 169346176 | bytes 23139612 | solution.py:62
  36.0 3.3 fusion.44
  39.5 6.5 %scatter_fusion = f32[29,128,128]{2,1,0:T(8,128)S(1)} fusion(f32[29,128,128]{2,1,0:T(8,128)S(1)} %broadcast.129, s32[40]{0:T(128)S(1)} %dynamic_slice.62, f32[40,128,128]{2,1,0:T(8,128)} %fusion.44), kind=kCustom, calls=%fused_computation.2.clone.clone.1 | custom fusion | flops 655360 | bytes 7864480 | tf_op jit(solution)/shard_map/while/body/eval_jaxpr/scatter-add | solution.py:58
  48.5 3.3 fusion.44
  52.1 6.5 %scatter_fusion = f32[29,128,128]{2,1,0:T(8,128)S(1)} fusion(f32[29,128,128]{2,1,0:T(8,128)S(1)} %broadcast.129, s32[40]{0:T(128)S(1)} %dynamic_slice.62, f32[40,128,128]{2,1,0:T(8,128)} %fusion.44), kind=kCustom, calls=%fused_computation.2.clone.clone.1 | custom fusion | flops 655360 | bytes 7864480 | tf_op jit(solution)/shard_map/while/body/eval_jaxpr/scatter-add | solution.py:58
  58.6 3.0 slice_add_fusion.4
  62.5 3.3 fusion.44
  66.1 6.5 %scatter_fusion = f32[29,128,128]{2,1,0:T(8,128)S(1)} fusion(f32[29,128,128]{2,1,0:T(8,128)S(1)} %broadcast.129, s32[40]{0:T(128)S(1)} %dynamic_slice.62, f32[40,128,128]{2,1,0:T(8,128)} %fusion.44), kind=kCustom, calls=%fused_computation.2.clone.clone.1 | custom fusion | flops 655360 | bytes 7864480 | tf_op jit(solution)/shard_map/while/body/eval_jaxpr/scatter-add | solution.py:58
  72.6 3.0 slice_add_fusion.4
  76.6 3.3 fusion.44
  80.1 6.5 %scatter_fusion = f32[29,128,128]{2,1,0:T(8,128)S(1)} fusion(f32[29,128,128]{2,1,0:T(8,128)S(1)} %broadcast.129, s32[40]{0:T(128)S(1)} %dynamic_slice.62, f32[40,128,128]{2,1,0:T(8,128)} %fusion.44), kind=kCustom, calls=%fused_computation.2.clone.clone.1 | custom fusion | flops 655360 | bytes 7864480 | tf_op jit(solution)/shard_map/while/body/eval_jaxpr/scatter-add | solution.py:58
  86.7 3.0 slice_add_fusion.4
  90.6 3.3 fusion.44
  94.1 6.5 %scatter_fusion = f32[29,128,128]{2,1,0:T(8,128)S(1)} fusion(f32[29,128,128]{2,1,0:T(8,128)S(1)} %broadcast.129, s32[40]{0:T(128)S(1)} %dynamic_slice.62, f32[40,128,128]{2,1,0:T(8,128)} %fusion.44), kind=kCustom, calls=%fused_computation.2.clone.clone.1 | custom fusion | flops 655360 | bytes 7864480 | tf_op jit(solution)/shard_map/while/body/eval_jaxpr/scatter-add | solution.py:58
  100.7 3.0 slice_add_fusion.4
  104.6 3.3 fusion.44
  108.2 6.5 %scatter_fusion = f32[29,128,128]{2,1,0:T(8,128)S(1)} fusion(f32[29,128,128]{2,1,0:T(8,128)S(1)} %broadcast.129, s32[40]{0:T(128)S(1)} %dynamic_slice.62, f32[40,128,128]{2,1,0:T(8,128)} %fusion.44), kind=kCustom, calls=%fused_computation.2.clone.clone.1 | custom fusion | flops 655360 | bytes 7864480 | tf_op jit(solution)/shard_map/while/body/eval_jaxpr/scatter-add | solution.py:58
  114.7 3.0 slice_add_fusion.4
  118.6 3.3 fusion.44
  122.2 6.5 %scatter_fusion = f32[29,128,128]{2,1,0:T(8,128)S(1)} fusion(f32[29,128,128]{2,1,0:T(8,128)S(1)} %broadcast.129, s32[40]{0:T(128)S(1)} %dynamic_slice.62, f32[40,128,128]{2,1,0:T(8,128)} %fusion.44), kind=kCustom, calls=%fused_computation.2.clone.clone.1 | custom fusion | flops 655360 | bytes 7864480 | tf_op jit(solution)/shard_map/while/body/eval_jaxpr/scatter-add | solution.py:58
  128.7 3.0 slice_add_fusion.4
  132.7 3.3 fusion.44
  136.2 6.5 %scatter_fusion = f32[29,128,128]{2,1,0:T(8,128)S(1)} fusion(f32[29,128,128]{2,1,0:T(8,128)S(1)} %broadcast.129, s32[40]{0:T(128)S(1)} %dynamic_slice.62, f32[40,128,128]{2,1,0:T(8,128)} %fusion.44), kind=kCustom, calls=%fused_computation.2.clone.clone.1 | custom fusion | flops 655360 | bytes 7864480 | tf_op jit(solution)/shard_map/while/body/eval_jaxpr/scatter-add | solution.py:58
  142.7 3.0 slice_add_fusion.4
  147.6 14.4 %copy.13 = bf16[1,1,320,128,128]{3,4,2,1,0:T(8,128)(2,1)} copy(bf16[1,1,320,128,128]{4,3,2,1,0:T(8,128)(2,1)} %bitcast.61) | data formatting | bytes 20971520 | tf_op args[2]
  164.3 2.6 collective-permute-start.2
  166.9 2.3 collective-permute-start.1
  170.2 3.5 collective-permute-done.4
  173.7 2.2 collective-permute-done.1
  177.4 1.8 collective-permute-start.11
  179.3 1.8 collective-permute-start.10
  181.1 3.4 collective-permute-start.9
  185.5 4.3 collective-permute-done.6
  189.8 3.4 collective-permute-start.7
  193.2 4.5 %collective-permute-done.7 = bf16[512,128]{1,0:T(8,128)(2,1)S(1)} collective-permute-done((bf16[512,128]{1,0:T(8,128)(2,1)S(1)}, bf16[512,128]{1,0:T(8,128)(2,1)S(1)}, u32[]{:S(2)}, u32[]{:S(2)}) %collective-permute-start.7) | collective-permute-done | bytes 131104 | tf_op jit(solution)/shard_map/ppermute | solution.py:11
  197.9 113.0 %while.29 = (s32[]{:T(128)}, f32[32,128,128]{2,1,0:T(8,128)}, s32[320]{0:T(512)S(1)}, bf16[320,128,128]{1,2,0:T(8,128)(2,1)}, s32[320]{0:T(512)S(1)}, /*index=5*...) while((s32[]{:T(128)}, f32[32,128,128]{2,1,0:T(8,128)}, ...), condition=%wide.region_5.6_spmd.clone, body=%wide.region_3.5_spmd.clone.sunk | while | flops 169477248 | bytes 24188188 | solution.py:62
  198.8 3.4 fusion.47
  202.4 6.6 %scatter_fusion.1 = f32[33,128,128]{2,1,0:T(8,128)S(1)} fusion(f32[33,128,128]{2,1,0:T(8,128)S(1)} %broadcast.136, s32[40]{0:T(128)S(1)} %dynamic_slice.65, f32[40,128,128]{2,1,0:T(8,128)} %fusion.47), kind=kCustom, calls=%fused_computation.3.clone.clone.1 | custom fusion | flops 655360 | bytes 7864480 | tf_op jit(solution)/shard_map/while/body/eval_jaxpr/scatter-add | solution.py:58
  211.6 3.4 fusion.47
  215.2 6.6 %scatter_fusion.1 = f32[33,128,128]{2,1,0:T(8,128)S(1)} fusion(f32[33,128,128]{2,1,0:T(8,128)S(1)} %broadcast.136, s32[40]{0:T(128)S(1)} %dynamic_slice.65, f32[40,128,128]{2,1,0:T(8,128)} %fusion.47), kind=kCustom, calls=%fused_computation.3.clone.clone.1 | custom fusion | flops 655360 | bytes 7864480 | tf_op jit(solution)/shard_map/while/body/eval_jaxpr/scatter-add | solution.py:58
  221.7 3.2 slice_add_fusion.5
  225.9 3.4 fusion.47
  229.5 6.6 %scatter_fusion.1 = f32[33,128,128]{2,1,0:T(8,128)S(1)} fusion(f32[33,128,128]{2,1,0:T(8,128)S(1)} %broadcast.136, s32[40]{0:T(128)S(1)} %dynamic_slice.65, f32[40,128,128]{2,1,0:T(8,128)} %fusion.47), kind=kCustom, calls=%fused_computation.3.clone.clone.1 | custom fusion | flops 655360 | bytes 7864480 | tf_op jit(solution)/shard_map/while/body/eval_jaxpr/scatter-add | solution.py:58
  236.1 3.2 slice_add_fusion.5
  240.3 3.4 fusion.47
  243.9 6.6 %scatter_fusion.1 = f32[33,128,128]{2,1,0:T(8,128)S(1)} fusion(f32[33,128,128]{2,1,0:T(8,128)S(1)} %broadcast.136, s32[40]{0:T(128)S(1)} %dynamic_slice.65, f32[40,128,128]{2,1,0:T(8,128)} %fusion.47), kind=kCustom, calls=%fused_computation.3.clone.clone.1 | custom fusion | flops 655360 | bytes 7864480 | tf_op jit(solution)/shard_map/while/body/eval_jaxpr/scatter-add | solution.py:58
  250.4 3.2 slice_add_fusion.5
  254.6 3.4 fusion.47
  258.2 6.6 %scatter_fusion.1 = f32[33,128,128]{2,1,0:T(8,128)S(1)} fusion(f32[33,128,128]{2,1,0:T(8,128)S(1)} %broadcast.136, s32[40]{0:T(128)S(1)} %dynamic_slice.65, f32[40,128,128]{2,1,0:T(8,128)} %fusion.47), kind=kCustom, calls=%fused_computation.3.clone.clone.1 | custom fusion | flops 655360 | bytes 7864480 | tf_op jit(solution)/shard_map/while/body/eval_jaxpr/scatter-add | solution.py:58
  264.7 3.2 slice_add_fusion.5
  268.9 3.3 fusion.47
  272.5 6.6 %scatter_fusion.1 = f32[33,128,128]{2,1,0:T(8,128)S(1)} fusion(f32[33,128,128]{2,1,0:T(8,128)S(1)} %broadcast.136, s32[40]{0:T(128)S(1)} %dynamic_slice.65, f32[40,128,128]{2,1,0:T(8,128)} %fusion.47), kind=kCustom, calls=%fused_computation.3.clone.clone.1 | custom fusion | flops 655360 | bytes 7864480 | tf_op jit(solution)/shard_map/while/body/eval_jaxpr/scatter-add | solution.py:58
  279.1 3.2 slice_add_fusion.5
  283.2 3.4 fusion.47
  286.8 6.5 %scatter_fusion.1 = f32[33,128,128]{2,1,0:T(8,128)S(1)} fusion(f32[33,128,128]{2,1,0:T(8,128)S(1)} %broadcast.136, s32[40]{0:T(128)S(1)} %dynamic_slice.65, f32[40,128,128]{2,1,0:T(8,128)} %fusion.47), kind=kCustom, calls=%fused_computation.3.clone.clone.1 | custom fusion | flops 655360 | bytes 7864480 | tf_op jit(solution)/shard_map/while/body/eval_jaxpr/scatter-add | solution.py:58
  293.4 3.2 slice_add_fusion.5
  297.5 3.4 fusion.47
  301.1 6.5 %scatter_fusion.1 = f32[33,128,128]{2,1,0:T(8,128)S(1)} fusion(f32[33,128,128]{2,1,0:T(8,128)S(1)} %broadcast.136, s32[40]{0:T(128)S(1)} %dynamic_slice.65, f32[40,128,128]{2,1,0:T(8,128)} %fusion.47), kind=kCustom, calls=%fused_computation.3.clone.clone.1 | custom fusion | flops 655360 | bytes 7864480 | tf_op jit(solution)/shard_map/while/body/eval_jaxpr/scatter-add | solution.py:58
  307.7 3.2 slice_add_fusion.5
  310.9 2.7 convert_element_type.108
  313.6 75.7 %psum.15 = f32[256]{0:T(256)S(1)} all-reduce(f32[256]{0:T(256)S(1)} %get-tuple-element.296), channel_id=1, replica_groups=mesh['rep'=8,'blk'=32] {'rep','blk'}, use_global_device_ids=true, to_apply=%region_9.10 | all-reduce | flops 256 | bytes 2048 | tf_op jit(solution)/shard_map/psum | solution.py:90
  389.9 38.9 %all-reduce.2.cloned.1.call-done = f32[128,256]{1,0:T(8,128)} async-done(((f32[128,256]{1,0:T(8,128)}), f32[128,256]{1,0:T(8,128)}) %all-reduce.2.cloned.1.call-update) | async-done | bytes 131088 | tf_op jit(solution)/shard_map/psum | solution.py:90
  (139 shorter events, 36.3 us)
Async XLA Ops:
  8.0 168.1 %copy-start = (bf16[128,256]{1,0:T(8,128)(2,1)S(1)}, bf16[128,256]{1,0:T(8,128)(2,1)}, u32[]{:S(2)}) copy-start(bf16[128,256]{1,0:T(8,128)(2,1)} %param.19) | copy-start | bytes 196612
  8.0 10.5 %copy-start.2 = (s32[1,1,320]{2,1,0:T(1,128)S(1)}, s32[1,1,320]{2,1,0:T(1,128)}, u32[]{:S(2)}) copy-start(s32[1,1,320]{2,1,0:T(1,128)} %param.17) | copy-start | bytes 3844
  8.0 10.5 %copy-start.3 = (s32[1,1,320]{2,1,0:T(1,128)S(1)}, s32[1,1,320]{2,1,0:T(1,128)}, u32[]{:S(2)}) copy-start(s32[1,1,320]{2,1,0:T(1,128)} %param.16) | copy-start | bytes 3844
  10.9 24.1 %all-to-all-start = ((bf16[8,512,128]{2,1,0:T(8,128)(2,1)}), bf16[8,512,128]{2,1,0:T(8,128)(2,1)S(1)}, u32[]{:S(2)}, u32[]{:S(2)}) async-start(bf16[8,512,128]{2,1,0:T(8,128)(2,1)} %stack.35), calls=%async_computation | async-start | bytes 2097152 | tf_op jit(solution)/shard_map/all_to_all | solution.py:67
  17.8 411.0 %all-reduce.2.cloned.1.call-start = ((), (), s32[]{:S(2)}) async-start(), calls=%async_computation.3 | async-start | bytes 262144 | tf_op jit(solution)/shard_map/psum | solution.py:90
  147.4 19.5 %collective-permute-start.5 = (bf16[512,128]{1,0:T(8,128)(2,1)S(1)}, bf16[512,128]{1,0:T(8,128)(2,1)S(1)}, u32[]{:S(2)}, u32[]{:S(2)}) collective-permute-start(bf16[512,128]{1,0:T(8,128)(2,1)S(1)} %bitcast.69), channel_id=1, source_target_pairs={{0,3},{1,4},{2,5},{3,6},{4,7},{5,8},{6,9},{7,10},{8,11},{9,12},{10... | collective-permute-start | bytes 393224 | tf_op jit(solution)/shard_map/ppermute | solution.py:11
  147.5 28.4 %copy-start.1 = (bf16[512,128]{1,0:T(8,128)(2,1)S(1)}, bf16[512,128]{1,0:T(8,128)(2,1)}, u32[]{:S(2)}) copy-start(bf16[512,128]{1,0:T(8,128)(2,1)} %param.13) | copy-start | bytes 393220
  147.5 28.5 %copy-start.4 = (bf16[512,256]{1,0:T(8,128)(2,1)S(1)}, bf16[512,256]{1,0:T(8,128)(2,1)}, u32[]{:S(2)}) copy-start(bf16[512,256]{1,0:T(8,128)(2,1)} %param.21) | copy-start | bytes 786436
  147.6 28.5 %copy-start.5 = (f32[256]{0:T(256)S(1)}, f32[256]{0:T(256)}, u32[]{:S(2)}) copy-start(f32[256]{0:T(256)} %param.20) | copy-start | bytes 3076
  162.0 8.2 %collective-permute-start = (bf16[512,128]{1,0:T(8,128)(2,1)S(1)}, bf16[512,128]{1,0:T(8,128)(2,1)S(1)}, u32[]{:S(2)}, u32[]{:S(2)}) collective-permute-start(bf16[512,128]{1,0:T(8,128)(2,1)S(1)} %bitcast.68), channel_id=1, source_target_pairs={{0,29},{1,30},{2,31},{3,0},{4,1},{5,2},{6,3},{7,4},{8,5},{9,6},{10... | collective-permute-start | bytes 393224 | tf_op jit(solution)/shard_map/ppermute | solution.py:11
  163.7 10.0 %collective-permute-start.4 = (bf16[512,128]{1,0:T(8,128)(2,1)S(1)}, bf16[512,128]{1,0:T(8,128)(2,1)S(1)}, u32[]{:S(2)}, u32[]{:S(2)}) collective-permute-start(bf16[512,128]{1,0:T(8,128)(2,1)S(1)} %bitcast.67), channel_id=1, source_target_pairs={{0,2},{1,3},{2,4},{3,5},{4,6},{5,7},{6,8},{7,9},{8,10},{9,11},{10,... | collective-permute-start | bytes 393224 | tf_op jit(solution)/shard_map/ppermute | solution.py:11
  164.3 9.4 %collective-permute-start.3 = (bf16[512,128]{1,0:T(8,128)(2,1)S(1)}, bf16[512,128]{1,0:T(8,128)(2,1)S(1)}, u32[]{:S(2)}, u32[]{:S(2)}) collective-permute-start(bf16[512,128]{1,0:T(8,128)(2,1)S(1)} %bitcast.66), channel_id=1, source_target_pairs={{0,1},{1,2},{2,3},{3,4},{4,5},{5,6},{6,7},{7,8},{8,9},{9,10},{10,1... | collective-permute-start | bytes 393224 | tf_op jit(solution)/shard_map/ppermute | solution.py:11
  164.3 9.4 %collective-permute-start.2 = (bf16[512,128]{1,0:T(8,128)(2,1)S(1)}, bf16[512,128]{1,0:T(8,128)(2,1)S(1)}, u32[]{:S(2)}, u32[]{:S(2)}) collective-permute-start(bf16[512,128]{1,0:T(8,128)(2,1)S(1)} %bitcast.65), channel_id=1, source_target_pairs={{0,31},{1,0},{2,1},{3,2},{4,3},{5,4},{6,5},{7,6},{8,7},{9,8},{10,9... | collective-permute-start | bytes 393224 | tf_op jit(solution)/shard_map/ppermute | solution.py:11
  166.9 9.0 %collective-permute-start.1 = (bf16[512,128]{1,0:T(8,128)(2,1)S(1)}, bf16[512,128]{1,0:T(8,128)(2,1)S(1)}, u32[]{:S(2)}, u32[]{:S(2)}) collective-permute-start(bf16[512,128]{1,0:T(8,128)(2,1)S(1)} %bitcast.64), channel_id=1, source_target_pairs={{0,30},{1,31},{2,0},{3,1},{4,2},{5,3},{6,4},{7,5},{8,6},{9,7},{10,... | collective-permute-start | bytes 393224 | tf_op jit(solution)/shard_map/ppermute | solution.py:11
  177.4 20.4 %collective-permute-start.11 = (bf16[512,128]{1,0:T(8,128)(2,1)S(1)}, bf16[512,128]{1,0:T(8,128)(2,1)S(1)}, u32[]{:S(2)}, u32[]{:S(2)}) collective-permute-start(bf16[512,128]{1,0:T(8,128)(2,1)S(1)} %fusion.6), channel_id=1, source_target_pairs={{0,29},{1,30},{2,31},{3,0},{4,1},{5,2},{6,3},{7,4},{8,5},{9,6},{10... | collective-permute-start | bytes 393224 | tf_op jit(solution)/shard_map/ppermute | solution.py:11
  179.3 18.5 %collective-permute-start.10 = (bf16[512,128]{1,0:T(8,128)(2,1)S(1)}, bf16[512,128]{1,0:T(8,128)(2,1)S(1)}, u32[]{:S(2)}, u32[]{:S(2)}) collective-permute-start(bf16[512,128]{1,0:T(8,128)(2,1)S(1)} %fusion.6), channel_id=1, source_target_pairs={{0,30},{1,31},{2,0},{3,1},{4,2},{5,3},{6,4},{7,5},{8,6},{9,7},{10,... | collective-permute-start | bytes 393224 | tf_op jit(solution)/shard_map/ppermute | solution.py:11
  181.1 16.6 %collective-permute-start.9 = (bf16[512,128]{1,0:T(8,128)(2,1)S(1)}, bf16[512,128]{1,0:T(8,128)(2,1)S(1)}, u32[]{:S(2)}, u32[]{:S(2)}) collective-permute-start(bf16[512,128]{1,0:T(8,128)(2,1)S(1)} %fusion.6), channel_id=1, source_target_pairs={{0,31},{1,0},{2,1},{3,2},{4,3},{5,4},{6,5},{7,6},{8,7},{9,8},{10,9... | collective-permute-start | bytes 393224 | tf_op jit(solution)/shard_map/ppermute | solution.py:11
  184.5 13.2 %collective-permute-start.8 = (bf16[512,128]{1,0:T(8,128)(2,1)S(1)}, bf16[512,128]{1,0:T(8,128)(2,1)S(1)}, u32[]{:S(2)}, u32[]{:S(2)}) collective-permute-start(bf16[512,128]{1,0:T(8,128)(2,1)S(1)} %fusion.6), channel_id=1, source_target_pairs={{0,1},{1,2},{2,3},{3,4},{4,5},{5,6},{6,7},{7,8},{8,9},{9,10},{10,1... | collective-permute-start | bytes 393224 | tf_op jit(solution)/shard_map/ppermute | solution.py:11
  184.5 5.3 %collective-permute-start.6 = (bf16[512,128]{1,0:T(8,128)(2,1)S(1)}, bf16[512,128]{1,0:T(8,128)(2,1)S(1)}, u32[]{:S(2)}, u32[]{:S(2)}) collective-permute-start(bf16[512,128]{1,0:T(8,128)(2,1)S(1)} %fusion.6), channel_id=1, source_target_pairs={{0,3},{1,4},{2,5},{3,6},{4,7},{5,8},{6,9},{7,10},{8,11},{9,12},{10... | collective-permute-start | bytes 393224 | tf_op jit(solution)/shard_map/ppermute | solution.py:11
  185.4 245.0 %reduce-scatter.2.cloned.1.call-start = ((), (), s32[]{:S(2)}) async-start(), calls=%async_computation.2 | async-start | bytes 1179648 | tf_op jit(solution)/shard_map/reduce_scatter | solution.py:101
  189.8 7.9 %collective-permute-start.7 = (bf16[512,128]{1,0:T(8,128)(2,1)S(1)}, bf16[512,128]{1,0:T(8,128)(2,1)S(1)}, u32[]{:S(2)}, u32[]{:S(2)}) collective-permute-start(bf16[512,128]{1,0:T(8,128)(2,1)S(1)} %fusion.6), channel_id=1, source_target_pairs={{0,2},{1,3},{2,4},{3,5},{4,6},{5,7},{6,8},{7,9},{8,10},{9,11},{10,... | collective-permute-start | bytes 393224 | tf_op jit(solution)/shard_map/ppermute | solution.py:11
Sparse Core Ops, SparseCore 0:
  185.5 243.2 all-reduce.1
Sparse Core Ops, SparseCore 1:
  313.7 76.2 reduce-scatter.1
